TPU v7x, 32 devices: a whole 2x2x4 slice. The times are simulated.
32 devices in a mesh: groups: 2 (over y), ctx: 4 (over x, core), head: 4 (over z).
Axes of the slice: x: 2, y: 2, z: 4, core: 2. Of those that a mesh axis runs over, the one named last changes fastest.
Arguments:
- context: bfloat16 [8192, 1024], P(('groups', 'ctx', 'head')), parts along dimension 0, may hold values from -6 to 6
- w_kv: bfloat16 [1024, 2048], replicated, may hold values from -0.1875 to 0.1875
- queries: bfloat16 [32, 64, 2048], P(('groups', 'head')), parts along dimension 0, may hold values from -400 to 400
- gain: float32 [1024], replicated, may hold values from 0.25 to 1.75
- w_out: bfloat16 [1024, 1024], P('head'), may hold values from -0.1875 to 0.1875
Outputs:
- latent_out: bfloat16 [4096, 1024], P(('groups', 'ctx', 'head')), parts along dimension 0
There are 2 independent parts, one for each index of `groups`. A program takes and returns all parts, laid end to end along the dimension named above; an argument that names none is the same for every part. Nothing has to cross between parts.
All inputs are finite; a program needn't handle non-finite values.
Results may differ from a plain program's by a relative error of at most 0.01575.
Values may be sent and summed in bfloat16 or wider, within the bound.
No kernel may reach another device: no remote copies, remote signals or barrier semaphores. Data moves between devices by JAX's collectives and lax.ppermute only.
A program may use at most 64 MiB of HBM per device.

v0:
```python
import math
import jax
import jax.numpy as jnp
from jax import lax
from jax.sharding import PartitionSpec as P

epsilon = 1e-06


def body(context, w_kv, queries, gain, w_out):
    heads_local, head_size, latents = queries.shape
    model_width = w_kv.shape[0]
    total_heads = w_kv.shape[1] // (2 * head_size)
    head_count = lax.axis_size("head")
    ctx_count = lax.axis_size("ctx")
    head_scale = 1.0 / math.sqrt(head_size)
    projected = jnp.dot(context, w_kv, preferred_element_type=jnp.float32).astype(jnp.bfloat16)
    projected = projected.reshape(context.shape[0], total_heads, 2 * head_size)
    regrouped = lax.all_to_all(projected, "head", split_axis=1, concat_axis=0, tiled=True)
    key_rows = regrouped[:, :, :head_size]
    value_rows = regrouped[:, :, head_size:]
    block_size = min(512, latents)
    block_count = latents // block_size
    query_blocks = queries.reshape(heads_local, head_size, block_count, block_size)

    def attend(position):
        query_block = lax.dynamic_index_in_dim(query_blocks, position, 2, keepdims=False)
        scores = (
            jnp.einsum("hdq,khd->hqk", query_block, key_rows, preferred_element_type=jnp.float32)
            * head_scale
        )
        highest = jnp.max(scores, axis=2)
        weights = jnp.exp(scores - highest[:, :, None])
        row_total = jnp.sum(weights, axis=2)
        summed = jnp.einsum(
            "hqk,khd->hqd",
            weights.astype(jnp.bfloat16),
            value_rows,
            preferred_element_type=jnp.float32,
        )
        return (highest, row_total, summed)

    maxima, totals, partials = lax.map(attend, jnp.arange(block_count))
    maxima = maxima.transpose(1, 0, 2).reshape(heads_local, latents)
    totals = totals.transpose(1, 0, 2).reshape(heads_local, latents)
    partials = partials.transpose(1, 0, 2, 3).reshape(heads_local, latents * head_size // 128, 128)
    ctx_rows = latents // ctx_count
    overall = lax.pmax(maxima, "ctx")
    factor = jnp.exp(maxima - overall)
    spread = partials.reshape(heads_local, latents, head_size) * factor[:, :, None]
    scaled = spread.reshape(heads_local, latents * head_size // 128, 128)
    sums_own, total_own = (
        lax.psum_scatter(
            scaled.astype(jnp.bfloat16), "ctx", scatter_dimension=1, tiled=True
        ).astype(jnp.float32),
        lax.psum_scatter(
            (totals * factor).astype(jnp.bfloat16), "ctx", scatter_dimension=1, tiled=True
        ).astype(jnp.float32),
    )
    sums_own = sums_own.reshape(heads_local, ctx_rows, head_size)
    attended = sums_own / total_own[:, :, None]
    own_rows = ctx_rows // head_count
    packed = attended.reshape(heads_local, head_count, own_rows * head_size)
    gathered = lax.all_to_all(
        packed.astype(jnp.bfloat16), "head", split_axis=1, concat_axis=0, tiled=True
    ).astype(packed.dtype)
    joined = (
        gathered.reshape(total_heads, own_rows, head_size)
        .transpose(1, 0, 2)
        .reshape(own_rows, model_width)
    )
    mean_square = jnp.sum(joined * joined, axis=1, keepdims=True) / model_width
    normed = (joined * gain[None, :] * lax.rsqrt(mean_square + epsilon)).astype(jnp.bfloat16)
    result = jnp.dot(
        normed,
        lax.all_gather(w_out, "head", axis=0, tiled=True),
        preferred_element_type=jnp.float32,
    )
    return result.astype(jnp.bfloat16)


def solution(mesh):
    return jax.shard_map(
        body,
        mesh=mesh,
        in_specs=(
            P(("groups", "ctx", "head"), None),
            P(),
            P(("groups", "head"), None, None),
            P(),
            P("head", None),
        ),
        out_specs=P(("groups", "ctx", "head"), None),
        check_vma=False,
    )
```

profile of v0, /device:TPU:0, one launch (start us, length us, event | category | flops | bytes accessed | tf_op | source)
XLA Modules:
  0.0 184.5 jit_solution(581980694861545381)
XLA Ops:
  7.4 1.0 copy-done
  8.4 3.4 %fusion.15 = bf16[32,16,8,128]{3,2,1,0:T(8,128)(2,1)S(1)} fusion(bf16[256,1024]{1,0:T(8,128)(2,1)S(1)} %copy-done, bf16[1024,2048]{1,0:T(8,128)(2,1)} %param.8), kind=kOutput, calls=%fused_computation.16 | convolution fusion | flops 1074266112 | bytes 5767168 | tf_op jit(solution)/shard_map/dot_general | solution.py:17
  11.9 1.3 copy.24
  13.1 6.3 %all-to-all-start = ((bf16[256,16,128]{2,0,1:T(8,128)(2,1)}), bf16[256,16,128]{2,0,1:T(8,128)(2,1)S(1)}, u32[]{:S(2)}, u32[]{:S(2)}) async-start(bf16[256,16,128]{2,0,1:T(8,128)(2,1)} %bitcast.58), calls=%async_computation | async-start | bytes 2097152 | tf_op jit(solution)/shard_map/all_to_all | solution.py:19
  19.5 1.3 copy.25
  20.8 24.4 %all-to-all-done = bf16[256,16,128]{2,0,1:T(8,128)(2,1)S(1)} async-done(((bf16[256,16,128]{2,0,1:T(8,128)(2,1)}), bf16[256,16,128]{2,0,1:T(8,128)(2,1)S(1)}, u32[]{:S(2)}, u32[]{:S(2)}) %all-to-all-start) | async-done | bytes 1048608 | tf_op jit(solution)/shard_map/all_to_all | solution.py:19
  45.2 1.5 copy.13
  46.7 2.6 %all_to_all.23 = bf16[1024,4,128]{0,2,1:T(8,128)(2,1)} reshape(bf16[4,256,4,128]{1,0,3,2:T(4,128)(2,1)} %copy.13) | data formatting | bytes 2097152 | tf_op jit(solution)/shard_map/all_to_all | solution.py:19
  49.2 1.3 fusion.18
  50.5 32.3 %while.14 = (s32[]{:T(128)}, f32[4,4,512]{2,1,0:T(4,128)S(1)}, f32[4,4,512]{2,1,0:T(4,128)S(1)}, f32[4,4,512,64]{2,3,1,0:T(8,128)}, s32[4]{0:T(128)S(1)}, /*inde...) while((s32[]{:T(128)}, f32[4,4,512]{2,1,0:T(4,128)S(1)}, ...), condition=%wide.region_3.4_spmd, body=%wide.region_0.3_spmd.sunk | while | flops 553644032 | bytes 27067044 | solution.py:43
  50.5 0.6 dynamic_slice.17
  52.8 1.4 multiply_reduce_fusion.3
  54.2 2.6 %fusion.34 = f32[4,4,512,64]{2,3,1,0:T(8,128)} fusion(f32[4,4,512,64]{2,3,1,0:T(8,128)} %get-tuple-element.163, s32[]{:T(128)} %get-tuple-element.160, bf16[1024,4,64]{0,2,1:T(8,128)(2,1)S(1)} %get-tuple-element.178, f32[4,512,1024]{2,1,0:T(8,128)S(1)} %get-tuple-element.145, f32[4,512]{1,0:T(4,128)S(1)} %get-tuple-element.146), kind=kOutput, calls=%fused_computation.6.clone.1 | convolution fusion | flops 274726912 | bytes 9445888 | tf_op jit(solution)/shard_map/while/body/eval_jaxpr/hqk,khd->hqd/dot_general | solution.py:35
  56.8 1.8 fusion.33
  58.6 0.6 dynamic_slice.17
  60.9 1.4 multiply_reduce_fusion.3
  62.3 2.6 %fusion.34 = f32[4,4,512,64]{2,3,1,0:T(8,128)} fusion(f32[4,4,512,64]{2,3,1,0:T(8,128)} %get-tuple-element.163, s32[]{:T(128)} %get-tuple-element.160, bf16[1024,4,64]{0,2,1:T(8,128)(2,1)S(1)} %get-tuple-element.178, f32[4,512,1024]{2,1,0:T(8,128)S(1)} %get-tuple-element.145, f32[4,512]{1,0:T(4,128)S(1)} %get-tuple-element.146), kind=kOutput, calls=%fused_computation.6.clone.1 | convolution fusion | flops 274726912 | bytes 9445888 | tf_op jit(solution)/shard_map/while/body/eval_jaxpr/hqk,khd->hqd/dot_general | solution.py:35
  64.9 1.8 fusion.33
  66.7 0.6 dynamic_slice.17
  69.0 1.4 multiply_reduce_fusion.3
  70.4 2.6 %fusion.34 = f32[4,4,512,64]{2,3,1,0:T(8,128)} fusion(f32[4,4,512,64]{2,3,1,0:T(8,128)} %get-tuple-element.163, s32[]{:T(128)} %get-tuple-element.160, bf16[1024,4,64]{0,2,1:T(8,128)(2,1)S(1)} %get-tuple-element.178, f32[4,512,1024]{2,1,0:T(8,128)S(1)} %get-tuple-element.145, f32[4,512]{1,0:T(4,128)S(1)} %get-tuple-element.146), kind=kOutput, calls=%fused_computation.6.clone.1 | convolution fusion | flops 274726912 | bytes 9445888 | tf_op jit(solution)/shard_map/while/body/eval_jaxpr/hqk,khd->hqd/dot_general | solution.py:35
  72.9 1.8 fusion.33
  74.8 0.6 dynamic_slice.17
  77.0 1.4 multiply_reduce_fusion.3
  78.4 2.6 %fusion.34 = f32[4,4,512,64]{2,3,1,0:T(8,128)} fusion(f32[4,4,512,64]{2,3,1,0:T(8,128)} %get-tuple-element.163, s32[]{:T(128)} %get-tuple-element.160, bf16[1024,4,64]{0,2,1:T(8,128)(2,1)S(1)} %get-tuple-element.178, f32[4,512,1024]{2,1,0:T(8,128)S(1)} %get-tuple-element.145, f32[4,512]{1,0:T(4,128)S(1)} %get-tuple-element.146), kind=kOutput, calls=%fused_computation.6.clone.1 | convolution fusion | flops 274726912 | bytes 9445888 | tf_op jit(solution)/shard_map/while/body/eval_jaxpr/hqk,khd->hqd/dot_general | solution.py:35
  81.0 1.8 fusion.33
  82.8 10.4 %pmax.7 = f32[4,2048]{1,0:T(4,128)S(1)} all-reduce(f32[4,2048]{1,0:T(4,128)S(1)} %bitcast.79), channel_id=1, replica_groups=mesh['groups'=2,'ctx'=4,'head'=4] {'ctx'}, use_global_device_ids=true, to_apply=%region_4.5 | all-reduce | flops 8192 | bytes 65536 | tf_op jit(solution)/shard_map/pmax | solution.py:48
  93.2 2.6 %mul.37 = f32[4,2048,64]{2,1,0:T(8,128)} broadcast(f32[4,2048]{1,0:T(4,128)S(1)} %get-tuple-element.85), dimensions={0,1} | broadcast | bytes 2129920 | tf_op jit(solution)/shard_map/mul | solution.py:50
  95.8 4.6 %mul.38 = f32[4,1024,128]{2,1,0:T(8,128)} reshape(f32[4,2048,64]{2,1,0:T(8,128)} %mul.37) | data formatting | bytes 4194304 | tf_op jit(solution)/shard_map/mul | solution.py:50
  100.5 3.8 %copy.15 = f32[4,4,512,64]{3,2,1,0:T(8,128)} copy(f32[4,4,512,64]{2,3,0,1:T(8,128)} %bitcast.75) | data formatting | bytes 4194304 | tf_op jit(solution)/shard_map/transpose | solution.py:46
  104.2 4.6 %reshape_reshape.3 = f32[4,1024,128]{2,1,0:T(8,128)} reshape(f32[4,4,512,64]{3,2,1,0:T(8,128)} %copy.15) | data formatting | bytes 4194304 | tf_op jit(solution)/shard_map/reshape;reshape | solution.py:50
  108.9 1.1 copy.18
  110.0 3.4 %multiply_convert_fusion = bf16[4,1024,128]{2,1,0:T(8,128)(2,1)} fusion(f32[4,1024,128]{2,1,0:T(8,128)} %reshape_reshape.3, f32[4,1024,128]{2,1,0:T(8,128)} %mul.38), kind=kLoop, calls=%fused_computation.15 | loop fusion | flops 1048576 | bytes 5242880 | tf_op jit(solution)/shard_map/convert_element_type | solution.py:54
  113.5 0.5 all-gather.2.cloned.1.call-update
  114.0 16.9 %reduce-scatter.7.cloned.1.call-done = bf16[512,4]{1,0:T(8,128)(2,1)} async-done(((bf16[2048,4]{1,0:T(8,128)(2,1)}), bf16[512,4]{1,0:T(8,128)(2,1)}) %reduce-scatter.7.cloned.1.call-update) | async-done | bytes 4112
  130.9 1.0 copy.19
  131.9 0.3 div.17
  132.3 0.4 div.18
  132.7 25.6 %reduce-scatter.5.cloned.1.call-done = bf16[4,256,128]{2,1,0:T(8,128)(2,1)} async-done(((bf16[4,1024,128]{2,1,0:T(8,128)(2,1)}), bf16[4,256,128]{2,1,0:T(8,128)(2,1)}) %reduce-scatter.5.cloned.1.call-update) | async-done | bytes 262160 | tf_op jit(solution)/shard_map/reduce_scatter | solution.py:53
  158.3 1.2 reshape.56
  159.4 0.1 divide_convert_fusion
  159.6 0.2 copy.16
  159.8 13.1 %all_to_all.27 = bf16[4,4,8192]{2,0,1:T(4,128)(2,1)S(1)} all-to-all(bf16[4,4,8192]{2,0,1:T(4,128)(2,1)S(1)} %copy.16), channel_id=1, replica_groups=mesh['groups'=2,'ctx'=4,'head'=4] {'head'}, dimensions={1} | all-to-all | bytes 524288 | tf_op jit(solution)/shard_map/all_to_all | solution.py:64
  172.9 0.5 reshape.57
  173.5 0.3 copy.17
  173.8 0.2 multiply_reduce_fusion.1
  174.0 0.2 fusion.17
  174.3 2.8 %convolution_convert_fusion.1 = bf16[128,1024]{1,0:T(8,128)(2,1)} fusion(bf16[128,1024]{0,1:T(8,128)(2,1)S(1)} %fusion.17, bf16[1024,1024]{1,0:T(8,128)(2,1)} %all-gather.2.cloned.1.call-done), kind=kOutput, calls=%fused_computation.17 | convolution fusion | flops 268566528 | bytes 2621440 | tf_op jit(solution)/shard_map/dot_general | solution.py:74
  (20 shorter events, 0.3 us)
Async XLA Ops:
  7.4 1.0 copy-start
  13.1 32.1 %all-to-all-start = ((bf16[256,16,128]{2,0,1:T(8,128)(2,1)}), bf16[256,16,128]{2,0,1:T(8,128)(2,1)S(1)}, u32[]{:S(2)}, u32[]{:S(2)}) async-start(bf16[256,16,128]{2,0,1:T(8,128)(2,1)} %bitcast.58), calls=%async_computation | async-start | bytes 2097152 | tf_op jit(solution)/shard_map/all_to_all | solution.py:19
  19.5 111.4 %reduce-scatter.7.cloned.1.call-start = ((), (), s32[]{:S(2)}) async-start(), calls=%async_computation.6 | async-start | bytes 655360
  109.9 48.3 %reduce-scatter.5.cloned.1.call-start = ((), (), s32[]{:S(2)}) async-start(), calls=%async_computation.4 | async-start | bytes 1310720 | tf_op jit(solution)/shard_map/reduce_scatter | solution.py:53
  113.5 60.8 %all-gather.2.cloned.1.call-start = ((), (), s32[]{:S(2)}) async-start(), calls=%async_computation.5 | async-start | bytes 2621440 | tf_op jit(solution)/shard_map/all_gather | solution.py:76
  132.7 41.3 %copy-start.1 = (f32[1024]{0:T(1024)S(1)}, f32[1024]{0:T(1024)}, u32[]{:S(2)}) copy-start(f32[1024]{0:T(1024)} %param.10) | copy-start | bytes 12292
Sparse Core Ops, SparseCore 0:
  110.1 20.8 reduce-scatter.6
  133.4 24.7 reduce-scatter.4
Sparse Core Ops, SparseCore 1:
  115.5 44.6 all-gather.1
where the time goes:
time: 185 us; the launch traced here: 184 us
  waiting for transfers between devices  67.4 us (36%)
  local copies, waits for them, and re-layouts  32 us (17%)
  blocking collectives  23.5 us (13%)
  matrix products  22.1 us (12%)
  between operations  15 us (8%)
  other arithmetic  11.3 us (6%)
  loops' own time  6.81 us (4%)
  starting transfers between devices  6.43 us (3%)
    reduce_scatter x1, waiting for transfers between devices, body(): lax.psum_scatter(scaled.astype(jnp.bfloat16), 'ctx', scatter_dimension=1,...  25.6 us
    all_to_all x1, waiting for transfers between devices, body(): lax.all_to_all(projected, 'head', split_axis=1, concat_axis=0, tiled=True)  24.4 us
    unnamed x4, waiting for transfers between devices  17.4 us
    all_to_all x1, blocking collectives, body(): lax.all_to_all(packed.astype(jnp.bfloat16), 'head', split_axis=1, concat_...  13.1 us
    pmax x1, blocking collectives, body(): overall = lax.pmax(maxima, 'ctx')  10.4 us
    dot_general x4, matrix products, attend(): jnp.einsum('hqk,khd->hqd', weights.astype(jnp.bfloat16), value_rows, pref...  10.3 us
    reduce_sum x4, other arithmetic, attend(): row_total = jnp.sum(weights, axis=2)  7.21 us
    mul x2, local copies, waits for them, and re-layouts, body(): partials.reshape(heads_local, latents, head_size) * factor[:, :, None]  7.21 us
  transfers between devices with their start and end apart: 4, of which 3 were waited for; matrix products, arithmetic and copies ran while one was open for 5% of the time, Pallas kernels for 0%

commit v1 on v0

--- a/solution.py
+++ b/solution.py
@@ -5,6 +5,22 @@
 from jax.sharding import PartitionSpec as P
 
 epsilon = 1e-06
+
+
+def swapped_with_each(x, axis, split, join):
+    ways, here = (lax.axis_size(axis), lax.axis_index(axis))
+    width = x.shape[split] // ways
+    shape = list(x.shape)
+    shape[split] = width
+    height = shape[join]
+    shape[join] = height * ways
+    full = jnp.zeros(shape, x.dtype)
+    for mask in range(ways):
+        part = lax.dynamic_slice_in_dim(x, (here ^ mask) * width, width, axis=split)
+        if mask:
+            part = lax.ppermute(part, axis, [(d, d ^ mask) for d in range(ways)])
+        full = lax.dynamic_update_slice_in_dim(full, part, (here ^ mask) * height, axis=join)
+    return full
 
 
 def body(context, w_kv, queries, gain, w_out):
@@ -16,7 +32,7 @@
     head_scale = 1.0 / math.sqrt(head_size)
     projected = jnp.dot(context, w_kv, preferred_element_type=jnp.float32).astype(jnp.bfloat16)
     projected = projected.reshape(context.shape[0], total_heads, 2 * head_size)
-    regrouped = lax.all_to_all(projected, "head", split_axis=1, concat_axis=0, tiled=True)
+    regrouped = swapped_with_each(projected, "head", 1, 0)
     key_rows = regrouped[:, :, :head_size]
     value_rows = regrouped[:, :, head_size:]
     block_size = min(512, latents)

time: 185 us -> 180 us (0.973)
  waiting for transfers between devices: 67.4 us -> 64 us
    all_to_all x1 -> x0, waiting for transfers between devices: 24.4 us -> none  [body(): lax.all_to_all(projected, 'head', split_axis=1, concat_axis=0, tiled=True)]
    ppermute x0 -> x3, waiting for transfers between devices: none -> 16.6 us  [swapped_with_each(): part = lax.ppermute(part, axis, [(d, d ^ mask) for d in range(ways)])]
    all_to_all x1 -> x0, starting transfers between devices: 6.35 us -> none  [body(): lax.all_to_all(projected, 'head', split_axis=1, concat_axis=0, tiled=True)]
    ppermute x0 -> x3, starting transfers between devices: none -> 5.63 us  [swapped_with_each(): part = lax.ppermute(part, axis, [(d, d ^ mask) for d in range(ways)])]
    unnamed x4, waiting for transfers between devices: 17.4 us -> 21.8 us
    all_to_all x2 -> x0, local copies, waits for them, and re-layouts: 4.04 us -> none  [body(): lax.all_to_all(projected, 'head', split_axis=1, concat_axis=0, tiled=True)]
    dynamic_update_slice x0 -> x3, local copies, waits for them, and re-layouts: none -> 2.22 us  [swapped_with_each(): lax.dynamic_update_slice_in_dim(full, part, (here ^ mask) * height, axis=...]
  transfers between devices with their start and end apart: 4 -> 6, of which waited for: 3 -> 4; matrix products, arithmetic and copies ran while one was open for 5% -> 6% of each run, Pallas kernels for 0% -> 0%
where the time goes in v1:
time: 180 us; the launch traced here: 179 us
  waiting for transfers between devices  64 us (36%)
  local copies, waits for them, and re-layouts  30.2 us (17%)
  blocking collectives  23.4 us (13%)
  matrix products  22.2 us (12%)
  between operations  15 us (8%)
  other arithmetic  10.6 us (6%)
  loops' own time  7.68 us (4%)
  starting transfers between devices  5.72 us (3%)
    reduce_scatter x1, waiting for transfers between devices, body(): lax.psum_scatter(scaled.astype(jnp.bfloat16), 'ctx', scatter_dimension=1,...  25.6 us
    unnamed x4, waiting for transfers between devices  21.8 us
    ppermute x3, waiting for transfers between devices, swapped_with_each(): part = lax.ppermute(part, axis, [(d, d ^ mask) for d in range(ways)])  16.6 us
    all_to_all x1, blocking collectives, body(): lax.all_to_all(packed.astype(jnp.bfloat16), 'head', split_axis=1, concat_...  13.1 us
    dot_general x4, matrix products, attend(): jnp.einsum('hqk,khd->hqd', weights.astype(jnp.bfloat16), value_rows, pref...  10.4 us
    pmax x1, blocking collectives, body(): overall = lax.pmax(maxima, 'ctx')  10.3 us
    another operation x1, loops' own time, body(): maxima, totals, partials = lax.map(attend, jnp.arange(block_count))  7.68 us
    reduce_sum x4, other arithmetic, attend(): row_total = jnp.sum(weights, axis=2)  7.21 us
  transfers between devices with their start and end apart: 6, of which 4 were waited for; matrix products, arithmetic and copies ran while one was open for 6% of the time, Pallas kernels for 0%

profile of v1, /device:TPU:0, one launch (start us, length us, event | category | flops | bytes accessed | tf_op | source)
XLA Modules:
  0.0 178.9 jit_solution(2697159791538923040)
XLA Ops:
  7.4 1.0 copy-done
  8.4 3.4 %convolution_convert_fusion = bf16[256,2048]{1,0:T(8,128)(2,1)S(1)} fusion(bf16[256,1024]{1,0:T(8,128)(2,1)S(1)} %copy-done, bf16[1024,2048]{1,0:T(8,128)(2,1)} %param.8), kind=kOutput, calls=%fused_computation.14 | convolution fusion | flops 1074266112 | bytes 5767168 | tf_op jit(solution)/shard_map/dot_general | solution.py:33
  11.9 0.5 copy.28
  12.4 1.1 broadcast_in_dim.23
  13.5 0.8 constant_dynamic-slice_fusion
  14.3 3.0 %collective-permute-start = (bf16[256,4,128]{0,2,1:T(8,128)(2,1)S(1)}, bf16[256,4,128]{0,2,1:T(8,128)(2,1)S(1)}, u32[]{:S(2)}, u32[]{:S(2)}) collective-permute-start(bf16[256,4,128]{0,2,1:T(8,128)(2,1)S(1)} %get-tuple-element.94), channel_id=1, source_target_pairs={{0,1},{1,0},{2,3},{3,2},{4,5},{5,4},{6,7},{7,6},{8,9},{9,8},{10,11... | collective-permute-start | bytes 786440 | tf_op jit(solution)/shard_map/ppermute | solution.py:21
  17.4 2.6 %collective-permute-start.1 = (bf16[256,4,128]{0,2,1:T(8,128)(2,1)S(1)}, bf16[256,4,128]{0,2,1:T(8,128)(2,1)S(1)}, u32[]{:S(2)}, u32[]{:S(2)}) collective-permute-start(bf16[256,4,128]{0,2,1:T(8,128)(2,1)S(1)} %get-tuple-element.93), channel_id=1, source_target_pairs={{0,2},{1,3},{2,0},{3,1},{4,6},{5,7},{6,4},{7,5},{8,10},{9,11},{10,... | collective-permute-start | bytes 786440 | tf_op jit(solution)/shard_map/ppermute | solution.py:21
  20.0 1.3 copy.31
  21.3 7.2 %collective-permute-done = bf16[256,4,128]{0,2,1:T(8,128)(2,1)S(1)} collective-permute-done((bf16[256,4,128]{0,2,1:T(8,128)(2,1)S(1)}, bf16[256,4,128]{0,2,1:T(8,128)(2,1)S(1)}, u32[]{:S(2)}, u32[]{:S(2)}) %collective-permute-start) | collective-permute-done | bytes 262176 | tf_op jit(solution)/shard_map/ppermute | solution.py:21
  28.6 0.7 constant_dynamic-update-slice_fusion.2
  29.3 9.4 %collective-permute-done.1 = bf16[256,4,128]{0,2,1:T(8,128)(2,1)S(1)} collective-permute-done((bf16[256,4,128]{0,2,1:T(8,128)(2,1)S(1)}, bf16[256,4,128]{0,2,1:T(8,128)(2,1)S(1)}, u32[]{:S(2)}, u32[]{:S(2)}) %collective-permute-start.1) | collective-permute-done | bytes 262176 | tf_op jit(solution)/shard_map/ppermute | solution.py:21
  38.7 0.8 constant_dynamic-update-slice_fusion.1
  39.4 0.7 constant_dynamic-update-slice_fusion
  40.2 1.3 fusion.17
  41.5 33.5 %while.14 = (s32[]{:T(128)}, f32[4,4,512]{2,1,0:T(4,128)S(1)}, f32[4,4,512]{2,1,0:T(4,128)S(1)}, f32[4,4,512,64]{2,3,1,0:T(8,128)}, s32[4]{0:T(128)S(1)}, /*inde...) while((s32[]{:T(128)}, f32[4,4,512]{2,1,0:T(4,128)S(1)}, ...), condition=%wide.region_3.4_spmd, body=%wide.region_0.3_spmd.sunk | while | flops 553644032 | bytes 27067044 | solution.py:59
  41.5 0.7 dynamic_slice.37
  44.1 1.4 multiply_reduce_fusion.3
  45.4 2.6 %fusion.33 = f32[4,4,512,64]{2,3,1,0:T(8,128)} fusion(f32[4,4,512,64]{2,3,1,0:T(8,128)} %get-tuple-element.167, s32[]{:T(128)} %get-tuple-element.164, bf16[1024,4,64]{0,2,1:T(8,128)(2,1)S(1)} %get-tuple-element.182, f32[4,512,1024]{2,1,0:T(8,128)S(1)} %get-tuple-element.149, f32[4,512]{1,0:T(4,128)S(1)} %get-tuple-element.150), kind=kOutput, calls=%fused_computation.6.clone.1 | convolution fusion | flops 274726912 | bytes 9445888 | tf_op jit(solution)/shard_map/while/body/eval_jaxpr/hqk,khd->hqd/dot_general | solution.py:51
  48.0 1.8 %fusion.32 = f32[4,512]{1,0:T(4,128)S(1)} fusion(f32[4,512,1024]{2,1,0:T(8,128)S(1)} %get-tuple-element.149, f32[4,512]{1,0:T(4,128)S(1)} %get-tuple-element.150), kind=kLoop, calls=%fused_computation.3.clone.1 | loop fusion | flops 6289408 | bytes 8404992 | tf_op jit(solution)/shard_map/while/body/eval_jaxpr/reduce_sum | solution.py:50
  49.9 0.7 dynamic_slice.37
  52.4 1.4 multiply_reduce_fusion.3
  53.8 2.6 %fusion.33 = f32[4,4,512,64]{2,3,1,0:T(8,128)} fusion(f32[4,4,512,64]{2,3,1,0:T(8,128)} %get-tuple-element.167, s32[]{:T(128)} %get-tuple-element.164, bf16[1024,4,64]{0,2,1:T(8,128)(2,1)S(1)} %get-tuple-element.182, f32[4,512,1024]{2,1,0:T(8,128)S(1)} %get-tuple-element.149, f32[4,512]{1,0:T(4,128)S(1)} %get-tuple-element.150), kind=kOutput, calls=%fused_computation.6.clone.1 | convolution fusion | flops 274726912 | bytes 9445888 | tf_op jit(solution)/shard_map/while/body/eval_jaxpr/hqk,khd->hqd/dot_general | solution.py:51
  56.4 1.8 %fusion.32 = f32[4,512]{1,0:T(4,128)S(1)} fusion(f32[4,512,1024]{2,1,0:T(8,128)S(1)} %get-tuple-element.149, f32[4,512]{1,0:T(4,128)S(1)} %get-tuple-element.150), kind=kLoop, calls=%fused_computation.3.clone.1 | loop fusion | flops 6289408 | bytes 8404992 | tf_op jit(solution)/shard_map/while/body/eval_jaxpr/reduce_sum | solution.py:50
  58.2 0.7 dynamic_slice.37
  60.8 1.4 multiply_reduce_fusion.3
  62.2 2.6 %fusion.33 = f32[4,4,512,64]{2,3,1,0:T(8,128)} fusion(f32[4,4,512,64]{2,3,1,0:T(8,128)} %get-tuple-element.167, s32[]{:T(128)} %get-tuple-element.164, bf16[1024,4,64]{0,2,1:T(8,128)(2,1)S(1)} %get-tuple-element.182, f32[4,512,1024]{2,1,0:T(8,128)S(1)} %get-tuple-element.149, f32[4,512]{1,0:T(4,128)S(1)} %get-tuple-element.150), kind=kOutput, calls=%fused_computation.6.clone.1 | convolution fusion | flops 274726912 | bytes 9445888 | tf_op jit(solution)/shard_map/while/body/eval_jaxpr/hqk,khd->hqd/dot_general | solution.py:51
  64.8 1.8 %fusion.32 = f32[4,512]{1,0:T(4,128)S(1)} fusion(f32[4,512,1024]{2,1,0:T(8,128)S(1)} %get-tuple-element.149, f32[4,512]{1,0:T(4,128)S(1)} %get-tuple-element.150), kind=kLoop, calls=%fused_computation.3.clone.1 | loop fusion | flops 6289408 | bytes 8404992 | tf_op jit(solution)/shard_map/while/body/eval_jaxpr/reduce_sum | solution.py:50
  66.6 0.7 dynamic_slice.37
  69.2 1.4 multiply_reduce_fusion.3
  70.6 2.6 %fusion.33 = f32[4,4,512,64]{2,3,1,0:T(8,128)} fusion(f32[4,4,512,64]{2,3,1,0:T(8,128)} %get-tuple-element.167, s32[]{:T(128)} %get-tuple-element.164, bf16[1024,4,64]{0,2,1:T(8,128)(2,1)S(1)} %get-tuple-element.182, f32[4,512,1024]{2,1,0:T(8,128)S(1)} %get-tuple-element.149, f32[4,512]{1,0:T(4,128)S(1)} %get-tuple-element.150), kind=kOutput, calls=%fused_computation.6.clone.1 | convolution fusion | flops 274726912 | bytes 9445888 | tf_op jit(solution)/shard_map/while/body/eval_jaxpr/hqk,khd->hqd/dot_general | solution.py:51
  73.2 1.8 %fusion.32 = f32[4,512]{1,0:T(4,128)S(1)} fusion(f32[4,512,1024]{2,1,0:T(8,128)S(1)} %get-tuple-element.149, f32[4,512]{1,0:T(4,128)S(1)} %get-tuple-element.150), kind=kLoop, calls=%fused_computation.3.clone.1 | loop fusion | flops 6289408 | bytes 8404992 | tf_op jit(solution)/shard_map/while/body/eval_jaxpr/reduce_sum | solution.py:50
  75.0 10.3 %pmax.7 = f32[4,2048]{1,0:T(4,128)S(1)} all-reduce(f32[4,2048]{1,0:T(4,128)S(1)} %bitcast.70), channel_id=1, replica_groups=mesh['groups'=2,'ctx'=4,'head'=4] {'ctx'}, use_global_device_ids=true, to_apply=%region_4.5 | all-reduce | flops 8192 | bytes 65536 | tf_op jit(solution)/shard_map/pmax | solution.py:64
  85.3 2.6 %mul.69 = f32[4,2048,64]{2,1,0:T(8,128)} broadcast(f32[4,2048]{1,0:T(4,128)S(1)} %get-tuple-element.85), dimensions={0,1} | broadcast | bytes 2129920 | tf_op jit(solution)/shard_map/mul | solution.py:66
  87.9 3.3 %mul.70 = f32[4,1024,128]{2,1,0:T(8,128)S(1)} reshape(f32[4,2048,64]{2,1,0:T(8,128)} %mul.69) | data formatting | bytes 4194304 | tf_op jit(solution)/shard_map/mul | solution.py:66
  91.1 3.8 %copy.23 = f32[4,4,512,64]{3,2,1,0:T(8,128)} copy(f32[4,4,512,64]{2,3,0,1:T(8,128)} %bitcast.66) | data formatting | bytes 4194304 | tf_op jit(solution)/shard_map/transpose | solution.py:62
  94.9 4.6 %reshape_reshape.3 = f32[4,1024,128]{2,1,0:T(8,128)} reshape(f32[4,4,512,64]{3,2,1,0:T(8,128)} %copy.23) | data formatting | bytes 4194304 | tf_op jit(solution)/shard_map/reshape;reshape | solution.py:66
  99.5 1.1 copy.26
  100.7 2.8 %multiply_convert_fusion = bf16[4,1024,128]{2,1,0:T(8,128)(2,1)} fusion(f32[4,1024,128]{2,1,0:T(8,128)} %reshape_reshape.3, f32[4,1024,128]{2,1,0:T(8,128)S(1)} %mul.70), kind=kLoop, calls=%fused_computation.15 | loop fusion | flops 1048576 | bytes 5242880 | tf_op jit(solution)/shard_map/convert_element_type | solution.py:70
  103.6 0.5 all-gather.2.cloned.1.call-update
  104.1 21.2 %reduce-scatter.7.cloned.1.call-done = bf16[512,4]{1,0:T(8,128)(2,1)} async-done(((bf16[2048,4]{1,0:T(8,128)(2,1)}), bf16[512,4]{1,0:T(8,128)(2,1)}) %reduce-scatter.7.cloned.1.call-update) | async-done | bytes 4112
  125.3 1.0 copy.27
  126.3 0.3 div.17
  126.7 0.4 div.18
  127.1 25.6 %reduce-scatter.5.cloned.1.call-done = bf16[4,256,128]{2,1,0:T(8,128)(2,1)} async-done(((bf16[4,1024,128]{2,1,0:T(8,128)(2,1)}), bf16[4,256,128]{2,1,0:T(8,128)(2,1)}) %reduce-scatter.5.cloned.1.call-update) | async-done | bytes 262160 | tf_op jit(solution)/shard_map/reduce_scatter | solution.py:69
  152.7 1.2 reshape.56
  154.2 13.1 %all_to_all.4 = bf16[4,4,8192]{2,0,1:T(4,128)(2,1)S(1)} all-to-all(bf16[4,4,8192]{2,0,1:T(4,128)(2,1)S(1)} %copy.24), channel_id=1, replica_groups=mesh['groups'=2,'ctx'=4,'head'=4] {'head'}, dimensions={1} | all-to-all | bytes 524288 | tf_op jit(solution)/shard_map/all_to_all | solution.py:80
  167.3 0.5 reshape.57
  168.7 2.8 %convolution_convert_fusion.1 = bf16[128,1024]{1,0:T(8,128)(2,1)} fusion(bf16[128,1024]{0,1:T(8,128)(2,1)S(1)} %fusion.16, bf16[1024,1024]{1,0:T(8,128)(2,1)} %all-gather.2.cloned.1.call-done), kind=kOutput, calls=%fused_computation.16 | convolution fusion | flops 268566528 | bytes 2621440 | tf_op jit(solution)/shard_map/dot_general | solution.py:90
  (27 shorter events, 1.4 us)
Async XLA Ops:
  7.4 1.0 copy-start
  7.4 117.9 %reduce-scatter.7.cloned.1.call-start = ((), (), s32[]{:S(2)}) async-start(), calls=%async_computation.5 | async-start | bytes 655360
  14.3 14.2 %collective-permute-start = (bf16[256,4,128]{0,2,1:T(8,128)(2,1)S(1)}, bf16[256,4,128]{0,2,1:T(8,128)(2,1)S(1)}, u32[]{:S(2)}, u32[]{:S(2)}) collective-permute-start(bf16[256,4,128]{0,2,1:T(8,128)(2,1)S(1)} %get-tuple-element.94), channel_id=1, source_target_pairs={{0,1},{1,0},{2,3},{3,2},{4,5},{5,4},{6,7},{7,6},{8,9},{9,8},{10,11... | collective-permute-start | bytes 786440 | tf_op jit(solution)/shard_map/ppermute | solution.py:21
  17.4 21.3 %collective-permute-start.1 = (bf16[256,4,128]{0,2,1:T(8,128)(2,1)S(1)}, bf16[256,4,128]{0,2,1:T(8,128)(2,1)S(1)}, u32[]{:S(2)}, u32[]{:S(2)}) collective-permute-start(bf16[256,4,128]{0,2,1:T(8,128)(2,1)S(1)} %get-tuple-element.93), channel_id=1, source_target_pairs={{0,2},{1,3},{2,0},{3,1},{4,6},{5,7},{6,4},{7,5},{8,10},{9,11},{10,... | collective-permute-start | bytes 786440 | tf_op jit(solution)/shard_map/ppermute | solution.py:21
  20.0 19.5 %collective-permute-start.2 = (bf16[256,4,128]{0,2,1:T(8,128)(2,1)S(1)}, bf16[256,4,128]{0,2,1:T(8,128)(2,1)S(1)}, u32[]{:S(2)}, u32[]{:S(2)}) collective-permute-start(bf16[256,4,128]{0,2,1:T(8,128)(2,1)S(1)} %get-tuple-element.92), channel_id=1, source_target_pairs={{0,3},{1,2},{2,1},{3,0},{4,7},{5,6},{6,5},{7,4},{8,11},{9,10},{10,... | collective-permute-start | bytes 786440 | tf_op jit(solution)/shard_map/ppermute | solution.py:21
  100.6 52.0 %reduce-scatter.5.cloned.1.call-start = ((), (), s32[]{:S(2)}) async-start(), calls=%async_computation.3 | async-start | bytes 1310720 | tf_op jit(solution)/shard_map/reduce_scatter | solution.py:69
  103.5 65.2 %all-gather.2.cloned.1.call-start = ((), (), s32[]{:S(2)}) async-start(), calls=%async_computation.4 | async-start | bytes 2621440 | tf_op jit(solution)/shard_map/all_gather | solution.py:92
  127.1 41.3 %copy-start.1 = (f32[1024]{0:T(1024)S(1)}, f32[1024]{0:T(1024)}, u32[]{:S(2)}) copy-start(f32[1024]{0:T(1024)} %param.10) | copy-start | bytes 12292
Sparse Core Ops, SparseCore 0:
  100.7 24.5 reduce-scatter.6
  127.8 24.7 reduce-scatter.4
Sparse Core Ops, SparseCore 1:
  105.5 48.4 all-gather.1
